TPU v7x, 512 devices: a whole 4x8x8 slice. The times are simulated.
512 devices in a mesh: row: 16 (over x, y_lo), col: 16 (over z, core), dp: 2 (over y_hi).
Axes of the slice: x: 4, y: 8 (y_hi: 2, y_lo: 4; y = y_hi * 4 + y_lo), z: 8, core: 2. Of those that a mesh axis runs over, the one named last changes fastest.
Arguments:
- grad_output: bfloat16 [2, 2048, 8192], P('dp', 'col', 'row'), may hold values from -0.09375 to 0.09375
- block_input: bfloat16 [2, 2048, 8192], P('dp', 'col', 'row'), may hold values from -6 to 6
- query_branch: bfloat16 [2, 2048, 8192], P('dp', 'row', 'col'), may hold values from -6 to 6
- key_branch: bfloat16 [2, 2048, 8192], P('dp', 'row', 'col'), may hold values from -6 to 6
- value_branch: bfloat16 [2, 2048, 8192], P('dp', 'row', 'col'), may hold values from -6 to 6
- out_weight: bfloat16 [8192, 8192], P('row', 'col'), may hold values from -0.0625 to 0.0625
- filters: float32 [512, 128], P('col'), may hold values from -0.5 to 0.5
Outputs:
- out_weight_grad: float32 [8192, 8192], P('row', 'col')
- value_weight_grad: float32 [8192, 8192], P('col', 'row')
- filter_grad: float32 [512, 128], P('col')
All inputs are finite; a program needn't handle non-finite values.
Results may differ from a plain program's by a relative error of at most 0.0029.
Values may be sent and summed in bfloat16 or wider, within the bound.
A program may use at most 128 MiB of HBM per device.

v0:
```python
import jax
import jax.numpy as jnp
from jax import lax
from jax.sharding import PartitionSpec as P

highest = lax.Precision.HIGHEST


def toeplitz(taps, tok_rows, causal):
    filter_len = taps.shape[1]
    out_pos = lax.broadcasted_iota(jnp.int32, (tok_rows, tok_rows + filter_len), 0)
    in_pos = lax.broadcasted_iota(jnp.int32, (tok_rows, tok_rows + filter_len), 1)
    lagged = out_pos + filter_len - in_pos if causal else in_pos - out_pos
    inside = (lagged >= 0) & (lagged < filter_len)
    picked = jnp.take(taps, jnp.clip(lagged, 0, filter_len - 1), axis=1)
    return jnp.where(inside[None], picked, 0.0)


def grouped_apply(table, signal, groups):
    blocks, extent, channels = signal.shape
    split = signal.reshape(blocks, extent, groups, channels // groups)
    result = jnp.einsum("gts,bsgc->btgc", table, split, precision=highest)
    return result.reshape(blocks, table.shape[1], channels)


def taps_partial(delta_mix, mixed_ext, groups, filter_len):
    blocks, tok_rows, channels = delta_mix.shape
    left_side = delta_mix.reshape(blocks, tok_rows, groups, channels // groups)
    right_side = mixed_ext.reshape(blocks, tok_rows + filter_len, groups, channels // groups)
    products = jnp.einsum("btgc,bsgc->gts", left_side, right_side, precision=highest)
    extent = tok_rows + filter_len
    flipped = products[:, :, ::-1]
    padded = jnp.pad(flipped, ((0, 0), (0, 0), (0, tok_rows)))
    flat_rows = padded.reshape(groups, -1)[:, : tok_rows * (extent + tok_rows - 1)]
    skewed = flat_rows.reshape(groups, tok_rows, extent + tok_rows - 1)
    column_sums = jnp.sum(skewed, axis=1)
    return column_sums[:, tok_rows - 1 : tok_rows - 1 + filter_len]


def local(grad_output, block_input, query_branch, key_branch, value_branch, out_weight, filters):
    filter_len = filters.shape[1]
    groups = filters.shape[0]
    tok_rows = query_branch.shape[1]
    channels = query_branch.shape[2]
    grads_all, inputs_all = (
        lax.all_gather(grad_output[0], "col", axis=0, tiled=True),
        lax.all_gather(block_input[0], "col", axis=0, tiled=True),
    )
    row_devices = lax.axis_size("row")
    sub_width = channels // row_devices
    delta_turned = lax.psum_scatter(
        lax.dot_general(
            out_weight, grads_all, (((0,), (1,)), ((), ())), preferred_element_type=jnp.float32
        ),
        "row",
        scatter_dimension=0,
        tiled=True,
    )
    queries, keys_here, values_here = (
        lax.all_to_all(query_branch[0], "row", split_axis=1, concat_axis=0, tiled=True),
        lax.all_to_all(key_branch[0], "row", split_axis=1, concat_axis=0, tiled=True),
        lax.all_to_all(value_branch[0], "row", split_axis=1, concat_axis=0, tiled=True),
    )
    delta_out = delta_turned.T
    local_groups = sub_width // (channels // groups)
    first_group = lax.axis_index("row") * local_groups
    my_taps = lax.dynamic_slice_in_dim(filters, first_group, local_groups, 0)
    mixed = keys_here.astype(jnp.float32) * values_here.astype(jnp.float32)
    mixed_blocks = mixed.reshape(row_devices, tok_rows, sub_width)
    earlier = jnp.concatenate(
        [
            jnp.zeros((1, filter_len, sub_width), jnp.float32),
            mixed_blocks[:-1, tok_rows - filter_len :],
        ],
        axis=0,
    )
    mixed_ext = jnp.concatenate([earlier, mixed_blocks], axis=1)
    conv_out = grouped_apply(toeplitz(my_taps, tok_rows, True), mixed_ext, local_groups).reshape(
        -1, sub_width
    )
    gated = (queries.astype(jnp.float32) * conv_out).astype(jnp.bfloat16)
    delta_mix = delta_out * queries.astype(jnp.float32)
    delta_blocks = delta_mix.reshape(row_devices, tok_rows, sub_width)
    later_part = jnp.concatenate(
        [delta_blocks[1:, :filter_len], jnp.zeros((1, filter_len, sub_width), jnp.float32)], axis=0
    )
    delta_ext = jnp.concatenate([delta_blocks, later_part], axis=1)
    delta_conv = grouped_apply(toeplitz(my_taps, tok_rows, False), delta_ext, local_groups).reshape(
        -1, sub_width
    )
    delta_value = (delta_conv * keys_here.astype(jnp.float32)).astype(jnp.bfloat16)
    my_terms = taps_partial(delta_blocks, mixed_ext, local_groups, filter_len)
    taps_local = lax.dynamic_update_slice_in_dim(
        jnp.zeros(filters.shape, jnp.float32), my_terms, first_group, 0
    )
    gated_all, value_all = (
        lax.all_gather(gated, "row", axis=1, tiled=True),
        lax.all_gather(delta_value, "row", axis=1, tiled=True),
    )
    out_grad = lax.dot_general(
        grads_all, gated_all, (((0,), (0,)), ((), ())), preferred_element_type=jnp.float32
    )
    value_grad = lax.dot_general(
        value_all, inputs_all, (((0,), (0,)), ((), ())), preferred_element_type=jnp.float32
    )
    out_grad, value_grad = lax.psum((out_grad, value_grad), "dp")
    taps_total = lax.psum(taps_local, ("row", "dp"))
    return (out_grad, value_grad, taps_total)


def solution(mesh):
    in_specs = (
        P("dp", "col", "row"),
        P("dp", "col", "row"),
        P("dp", "row", "col"),
        P("dp", "row", "col"),
        P("dp", "row", "col"),
        P("row", "col"),
        P("col", None),
    )
    out_specs = (P("row", "col"), P("col", "row"), P("col", None))
    return jax.shard_map(local, mesh=mesh, in_specs=in_specs, out_specs=out_specs, check_vma=False)
```

profile of v0, /device:TPU:64, one launch (start us, length us, event | category | flops | bytes accessed | tf_op | source)
XLA Modules:
  0.0 689.4 jit_solution(379694975442089937)
XLA Ops:
  7.2 0.7 all-gather.11.cloned.1.call-update
  8.0 48.5 %all-gather.11.cloned.1.call-done = bf16[1,2048,512]{2,1,0:T(8,128)(2,1)} async-done(((bf16[1,128,512]{2,1,0:T(8,128)(2,1)}), bf16[1,2048,512]{2,1,0:T(8,128)(2,1)}) %all-gather.11.cloned.1.call-update) | async-done | bytes 2097168 | tf_op jit(solution)/shard_map/all_gather | solution.py:46
  56.5 4.8 fusion.2
  61.4 0.9 copy-done.2
  62.2 0.8 copy.40
  63.0 7.1 %all-to-all-start.2 = ((bf16[128,16,32]{0,2,1:T(8,128)(2,1)}), bf16[128,16,32]{0,2,1:T(8,128)(2,1)S(1)}, u32[]{:S(2)}, u32[]{:S(2)}) async-start(bf16[128,16,32]{0,2,1:T(8,128)(2,1)} %bitcast.4), calls=%async_computation.2 | async-start | bytes 262144 | tf_op jit(solution)/shard_map/all_to_all | solution.py:62
  70.1 0.1 fusion.30
  70.3 0.1 copy.66
  70.4 0.7 constant_dynamic-slice_fusion
  71.1 0.8 copy.38
  71.8 0.1 copy.62
  71.9 109.0 %gather_fusion = f32[32768,2]{1,0:T(8,128)} fusion(f32[2,128]{0,1:T(8,128)S(1)} %copy.62, s32[32768]{0:T(1024)S(1)} %broadcast_clamp_fusion.1), kind=kCustom, calls=%fused_computation.clone | custom fusion | bytes 655360 | tf_op jit(solution)/shard_map/jit(_take)/gather | solution.py:15
  180.9 10.0 %copy.46 = f32[128,256,2]{1,0,2:T(8,128)S(1)} copy(f32[128,256,2]{2,1,0:T(8,128)} %bitcast.113) | data formatting | bytes 524288 | tf_op jit(solution)/shard_map/jit(_take)/gather | solution.py:15
  190.9 0.8 copy.36
  191.7 0.2 fusion.35
  191.9 7.5 %all-to-all-start.1 = ((bf16[128,16,32]{0,2,1:T(8,128)(2,1)}), bf16[128,16,32]{0,2,1:T(8,128)(2,1)S(1)}, u32[]{:S(2)}, u32[]{:S(2)}) async-start(bf16[128,16,32]{0,2,1:T(8,128)(2,1)} %bitcast.2), calls=%async_computation.1 | async-start | bytes 262144 | tf_op jit(solution)/shard_map/all_to_all | solution.py:61
  199.4 8.4 %all-to-all-done.1 = bf16[128,16,32]{0,2,1:T(8,128)(2,1)S(1)} async-done(((bf16[128,16,32]{0,2,1:T(8,128)(2,1)}), bf16[128,16,32]{0,2,1:T(8,128)(2,1)S(1)}, u32[]{:S(2)}, u32[]{:S(2)}) %all-to-all-start.1) | async-done | bytes 131104 | tf_op jit(solution)/shard_map/all_to_all | solution.py:61
  207.8 3.5 all-to-all-start
  211.3 0.0 all-gather.7.cloned.1.call-start
  211.4 0.1 slice.19
  211.5 0.1 copy_dynamic-update-slice_fusion
  211.7 0.6 convolution_bitcast_fusion.2
  212.3 0.1 copy.47
  212.4 7.3 %all-to-all-done = bf16[128,16,32]{0,2,1:T(8,128)(2,1)S(1)} async-done(((bf16[128,16,32]{0,2,1:T(8,128)(2,1)}), bf16[128,16,32]{0,2,1:T(8,128)(2,1)S(1)}, u32[]{:S(2)}, u32[]{:S(2)}) %all-to-all-start) | async-done | bytes 131104 | tf_op jit(solution)/shard_map/all_to_all | solution.py:60
  219.6 1.7 bitcast_multiply_fusion.2
  221.4 0.5 all-gather.13.cloned.1.call-update
  222.0 0.1 copy.69
  222.2 109.0 %gather_fusion.1 = f32[32768,2]{1,0:T(8,128)} fusion(f32[2,128]{0,1:T(8,128)S(1)} %copy.62, s32[32768]{0:T(1024)S(1)} %broadcast_clamp_fusion), kind=kCustom, calls=%fused_computation.1.clone | custom fusion | bytes 655360 | tf_op jit(solution)/shard_map/jit(_take)/gather | solution.py:15
  331.2 10.1 %copy.51 = f32[128,256,2]{1,0,2:T(8,128)S(1)} copy(f32[128,256,2]{2,1,0:T(8,128)} %bitcast.112) | data formatting | bytes 524288 | tf_op jit(solution)/shard_map/jit(_take)/gather | solution.py:15
  341.2 0.1 fusion.34
  341.3 0.1 slice.21
  341.4 0.1 copy.50
  341.6 0.1 copy.49
  341.7 0.6 convolution_bitcast_fusion.1
  342.3 0.1 copy.52
  342.4 0.7 fusion.13
  343.2 4.5 fusion.6
  347.7 1.5 all-gather.13.cloned.1.call-done
  349.2 91.4 %all-gather.9.cloned.1.call-done = bf16[2048,512]{0,1:T(8,128)(2,1)} async-done(((bf16[2048,32]{0,1:T(8,128)(2,1)}), bf16[2048,512]{0,1:T(8,128)(2,1)}) %all-gather.9.cloned.1.call-update) | async-done | bytes 2097168 | tf_op jit(solution)/shard_map/all_gather | solution.py:98
  440.6 4.4 fusion
  445.1 0.8 convolution_bitcast_fusion
  445.9 0.4 rev.3
  446.3 0.3 copy.71
  446.7 0.6 reshape.76
  447.3 0.1 slice_dynamic-update-slice_fusion
  447.4 231.5 %psum.23 = f32[32,128]{1,0:T(8,128)} all-reduce(f32[32,128]{1,0:T(8,128)S(1)} %slice_dynamic-update-slice_fusion), channel_id=1, replica_groups=mesh['row'=16,'col'=16,'dp'=2] {'row','dp'}, use_global_device_ids=true, to_apply=%region_4.6 | all-reduce | flops 4096 | bytes 32768 | tf_op jit(solution)/shard_map/psum | solution.py:107
  678.9 2.6 copy.54
  681.5 1.0 copy.88
  (39 shorter events, 0.7 us)
Async XLA Ops:
  7.2 49.3 %copy-start = (bf16[512,512]{1,0:T(8,128)(2,1)S(1)}, bf16[512,512]{1,0:T(8,128)(2,1)}, u32[]{:S(2)}) copy-start(bf16[512,512]{1,0:T(8,128)(2,1)} %param.14) | copy-start | bytes 1572868
  7.2 49.3 %all-gather.11.cloned.1.call-start = ((), (), s32[]{:S(2)}) async-start(), calls=%async_computation.7 | async-start | bytes 2228224 | tf_op jit(solution)/shard_map/all_gather | solution.py:46
  7.9 211.7 %reduce-scatter.2.cloned.1.call-start = ((), (), s32[]{:S(2)}) async-start(), calls=%async_computation.5 | async-start | bytes 4456448 | tf_op jit(solution)/shard_map/reduce_scatter | solution.py:51
  61.3 0.9 copy-start.2
  61.3 9.7 %copy-start.3 = (bf16[1,128,512]{2,1,0:T(8,128)(2,1)S(1)}, bf16[1,128,512]{2,1,0:T(8,128)(2,1)}, u32[]{:S(2)}) copy-start(bf16[1,128,512]{2,1,0:T(8,128)(2,1)} %param.12) | copy-start | bytes 393220
  63.0 128.9 %all-to-all-start.2 = ((bf16[128,16,32]{0,2,1:T(8,128)(2,1)}), bf16[128,16,32]{0,2,1:T(8,128)(2,1)S(1)}, u32[]{:S(2)}, u32[]{:S(2)}) async-start(bf16[128,16,32]{0,2,1:T(8,128)(2,1)} %bitcast.4), calls=%async_computation.2 | async-start | bytes 262144 | tf_op jit(solution)/shard_map/all_to_all | solution.py:62
  180.9 10.0 %copy-start.4 = (bf16[1,128,512]{2,1,0:T(8,128)(2,1)S(1)}, bf16[1,128,512]{2,1,0:T(8,128)(2,1)}, u32[]{:S(2)}) copy-start(bf16[1,128,512]{2,1,0:T(8,128)(2,1)} %param.11) | copy-start | bytes 393220
  191.9 15.9 %all-to-all-start.1 = ((bf16[128,16,32]{0,2,1:T(8,128)(2,1)}), bf16[128,16,32]{0,2,1:T(8,128)(2,1)S(1)}, u32[]{:S(2)}, u32[]{:S(2)}) async-start(bf16[128,16,32]{0,2,1:T(8,128)(2,1)} %bitcast.2), calls=%async_computation.1 | async-start | bytes 262144 | tf_op jit(solution)/shard_map/all_to_all | solution.py:61
  207.8 11.9 %all-to-all-start = ((bf16[128,16,32]{0,2,1:T(8,128)(2,1)}), bf16[128,16,32]{0,2,1:T(8,128)(2,1)S(1)}, u32[]{:S(2)}, u32[]{:S(2)}) async-start(bf16[128,16,32]{0,2,1:T(8,128)(2,1)} %bitcast), calls=%async_computation | async-start | bytes 262144 | tf_op jit(solution)/shard_map/all_to_all | solution.py:60
  211.3 131.9 %all-gather.7.cloned.1.call-start = ((), (), s32[]{:S(2)}) async-start(), calls=%async_computation.4 | async-start | bytes 2228224 | tf_op jit(solution)/shard_map/all_gather | solution.py:97
  221.4 127.9 %all-gather.13.cloned.1.call-start = ((), (), s32[]{:S(2)}) async-start(), calls=%async_computation.8 | async-start | bytes 2228224 | tf_op jit(solution)/shard_map/all_gather | solution.py:47
  222.0 218.7 %all-gather.9.cloned.1.call-start = ((), (), s32[]{:S(2)}) async-start(), calls=%async_computation.6 | async-start | bytes 2228224 | tf_op jit(solution)/shard_map/all_gather | solution.py:98
  343.2 335.8 %all-reduce.6.cloned.1.call-start = ((), (), s32[]{:S(2)}) async-start(), calls=%async_computation.9 | async-start | bytes 4194304 | tf_op jit(solution)/shard_map/psum | solution.py:106
  678.9 2.6 copy-start.1
Sparse Core Ops, SparseCore 0:
  10.1 46.3 all-gather.10
  61.5 105.1 reduce-scatter.1
  221.5 84.2 all-gather.6
  307.8 41.4 all-gather.12
  351.7 88.8 all-gather.8
  445.2 122.4 all-reduce.5
where the time goes:
time: 690 us; the launch traced here: 689 us
  local copies, waits for them, and re-layouts  248 us (36%)
  blocking collectives  232 us (34%)
  waiting for transfers between devices  158 us (23%)
  starting transfers between devices  18.4 us (3%)
  matrix products  15.8 us (2%)
  between operations  14.4 us (2%)
    gather x4, local copies, waits for them, and re-layouts, toeplitz(): picked = jnp.take(taps, jnp.clip(lagged, 0, filter_len - 1), axis=1)  238 us
    psum x1, blocking collectives, local(): taps_total = lax.psum(taps_local, ('row', 'dp'))  232 us
    all_gather x1, waiting for transfers between devices, local(): lax.all_gather(delta_value, 'row', axis=1, tiled=True)  91.4 us
    all_gather x1, waiting for transfers between devices, local(): lax.all_gather(grad_output[0], 'col', axis=0, tiled=True)  48.5 us
  transfers between devices with their start and end apart: 9, of which 5 were waited for; matrix products, arithmetic and copies ran while one was open for 36% of the time, Pallas kernels for 0%

commit v1 on v0

--- a/solution.py
+++ b/solution.py
@@ -104,7 +104,7 @@
         value_all, inputs_all, (((0,), (0,)), ((), ())), preferred_element_type=jnp.float32
     )
     out_grad, value_grad = lax.psum((out_grad, value_grad), "dp")
-    taps_total = lax.psum(taps_local, ("row", "dp"))
+    taps_total = jnp.sum(lax.all_gather(taps_local, ("row", "dp")), axis=0)
     return (out_grad, value_grad, taps_total)
 
 

time: 690 us -> 631 us (0.914)
  blocking collectives: 232 us -> 171 us
    psum x1 -> x0, blocking collectives: 232 us -> none  [local(): taps_total = lax.psum(taps_local, ('row', 'dp'))]
    all_gather x0 -> x1, blocking collectives: none -> 171 us  [local(): taps_total = jnp.sum(lax.all_gather(taps_local, ('row', 'dp')), axis=0)]
  transfers between devices with their start and end apart: 9 -> 9, of which waited for: 5 -> 5; matrix products, arithmetic and copies ran while one was open for 36% -> 40% of each run, Pallas kernels for 0% -> 0%
where the time goes in v1:
time: 631 us; the launch traced here: 630 us
  local copies, waits for them, and re-layouts  248 us (39%)
  blocking collectives  171 us (27%)
  waiting for transfers between devices  158 us (25%)
  starting transfers between devices  18.4 us (3%)
  matrix products  15.8 us (3%)
  between operations  14.4 us (2%)
    gather x4, local copies, waits for them, and re-layouts, toeplitz(): picked = jnp.take(taps, jnp.clip(lagged, 0, filter_len - 1), axis=1)  238 us
    all_gather x1, blocking collectives, local(): taps_total = jnp.sum(lax.all_gather(taps_local, ('row', 'dp')), axis=0)  171 us
    all_gather x1, waiting for transfers between devices, local(): lax.all_gather(delta_value, 'row', axis=1, tiled=True)  91.4 us
    all_gather x1, waiting for transfers between devices, local(): lax.all_gather(grad_output[0], 'col', axis=0, tiled=True)  48.5 us
  transfers between devices with their start and end apart: 9, of which 5 were waited for; matrix products, arithmetic and copies ran while one was open for 40% of the time, Pallas kernels for 0%

profile of v1, /device:TPU:64, one launch (start us, length us, event | category | flops | bytes accessed | tf_op | source)
XLA Modules:
  0.0 629.9 jit_solution(17899778265998381966)
XLA Ops:
  7.2 0.7 all-gather.11.cloned.1.call-update
  8.0 48.5 %all-gather.11.cloned.1.call-done = bf16[1,2048,512]{2,1,0:T(8,128)(2,1)} async-done(((bf16[1,128,512]{2,1,0:T(8,128)(2,1)}), bf16[1,2048,512]{2,1,0:T(8,128)(2,1)}) %all-gather.11.cloned.1.call-update) | async-done | bytes 2097168 | tf_op jit(solution)/shard_map/all_gather | solution.py:46
  56.5 4.8 fusion.2
  61.4 0.9 copy-done.2
  62.2 0.8 copy.59
  63.0 7.1 %all-to-all-start.2 = ((bf16[128,16,32]{0,2,1:T(8,128)(2,1)}), bf16[128,16,32]{0,2,1:T(8,128)(2,1)S(1)}, u32[]{:S(2)}, u32[]{:S(2)}) async-start(bf16[128,16,32]{0,2,1:T(8,128)(2,1)} %bitcast.4), calls=%async_computation.2 | async-start | bytes 262144 | tf_op jit(solution)/shard_map/all_to_all | solution.py:62
  70.1 0.1 fusion.30
  70.3 0.1 copy.85
  70.4 0.7 constant_dynamic-slice_fusion
  71.1 0.8 copy.57
  71.8 0.1 copy.81
  71.9 109.0 %gather_fusion = f32[32768,2]{1,0:T(8,128)} fusion(f32[2,128]{0,1:T(8,128)S(1)} %copy.81, s32[32768]{0:T(1024)S(1)} %broadcast_clamp_fusion.1), kind=kCustom, calls=%fused_computation.clone | custom fusion | bytes 655360 | tf_op jit(solution)/shard_map/jit(_take)/gather | solution.py:15
  180.9 10.0 %copy.65 = f32[128,256,2]{1,0,2:T(8,128)S(1)} copy(f32[128,256,2]{2,1,0:T(8,128)} %bitcast.117) | data formatting | bytes 524288 | tf_op jit(solution)/shard_map/jit(_take)/gather | solution.py:15
  190.9 0.8 copy.55
  191.7 0.2 fusion.35
  191.9 7.5 %all-to-all-start.1 = ((bf16[128,16,32]{0,2,1:T(8,128)(2,1)}), bf16[128,16,32]{0,2,1:T(8,128)(2,1)S(1)}, u32[]{:S(2)}, u32[]{:S(2)}) async-start(bf16[128,16,32]{0,2,1:T(8,128)(2,1)} %bitcast.2), calls=%async_computation.1 | async-start | bytes 262144 | tf_op jit(solution)/shard_map/all_to_all | solution.py:61
  199.4 8.4 %all-to-all-done.1 = bf16[128,16,32]{0,2,1:T(8,128)(2,1)S(1)} async-done(((bf16[128,16,32]{0,2,1:T(8,128)(2,1)}), bf16[128,16,32]{0,2,1:T(8,128)(2,1)S(1)}, u32[]{:S(2)}, u32[]{:S(2)}) %all-to-all-start.1) | async-done | bytes 131104 | tf_op jit(solution)/shard_map/all_to_all | solution.py:61
  207.8 3.5 all-to-all-start
  211.4 0.1 slice.19
  211.5 0.1 copy_dynamic-update-slice_fusion
  211.7 0.6 convolution_bitcast_fusion.2
  212.3 0.1 copy.66
  212.4 7.3 %all-to-all-done = bf16[128,16,32]{0,2,1:T(8,128)(2,1)S(1)} async-done(((bf16[128,16,32]{0,2,1:T(8,128)(2,1)}), bf16[128,16,32]{0,2,1:T(8,128)(2,1)S(1)}, u32[]{:S(2)}, u32[]{:S(2)}) %all-to-all-start) | async-done | bytes 131104 | tf_op jit(solution)/shard_map/all_to_all | solution.py:60
  219.6 1.7 bitcast_multiply_fusion.2
  221.4 0.5 all-gather.13.cloned.1.call-update
  222.0 0.1 copy.88
  222.2 109.0 %gather_fusion.1 = f32[32768,2]{1,0:T(8,128)} fusion(f32[2,128]{0,1:T(8,128)S(1)} %copy.81, s32[32768]{0:T(1024)S(1)} %broadcast_clamp_fusion), kind=kCustom, calls=%fused_computation.1.clone | custom fusion | bytes 655360 | tf_op jit(solution)/shard_map/jit(_take)/gather | solution.py:15
  331.2 10.1 %copy.70 = f32[128,256,2]{1,0,2:T(8,128)S(1)} copy(f32[128,256,2]{2,1,0:T(8,128)} %bitcast.116) | data formatting | bytes 524288 | tf_op jit(solution)/shard_map/jit(_take)/gather | solution.py:15
  341.2 0.1 fusion.34
  341.3 0.1 slice.21
  341.4 0.1 copy.69
  341.6 0.1 copy.68
  341.7 0.6 convolution_bitcast_fusion.1
  342.3 0.1 copy.71
  342.4 0.7 fusion.13
  343.2 4.5 fusion.6
  347.7 1.5 all-gather.13.cloned.1.call-done
  349.2 91.4 %all-gather.9.cloned.1.call-done = bf16[2048,512]{0,1:T(8,128)(2,1)} async-done(((bf16[2048,32]{0,1:T(8,128)(2,1)}), bf16[2048,512]{0,1:T(8,128)(2,1)}) %all-gather.9.cloned.1.call-update) | async-done | bytes 2097168 | tf_op jit(solution)/shard_map/all_gather | solution.py:98
  440.6 4.4 fusion
  445.1 0.8 convolution_bitcast_fusion
  445.9 0.4 rev.3
  446.3 0.3 copy.90
  446.7 0.6 reshape.78
  447.3 0.1 fusion.41
  447.4 171.4 %all_gather.23 = f32[32,32,128]{2,1,0:T(8,128)S(1)} all-gather(f32[1,32,128]{2,1,0:T(8,128)S(1)} %fusion.41), channel_id=1, replica_groups=mesh['row'=16,'col'=16,'dp'=2] {'row','dp'}, dimensions={0}, use_global_device_ids=true | all-gather | bytes 540672 | tf_op jit(solution)/shard_map/all_gather | solution.py:107
  618.8 0.6 reduce_sum.19
  619.5 2.6 copy.73
  622.1 1.0 copy.107
  (40 shorter events, 0.8 us)
Async XLA Ops:
  7.2 49.3 %copy-start = (bf16[512,512]{1,0:T(8,128)(2,1)S(1)}, bf16[512,512]{1,0:T(8,128)(2,1)}, u32[]{:S(2)}) copy-start(bf16[512,512]{1,0:T(8,128)(2,1)} %param.14) | copy-start | bytes 1572868
  7.2 49.3 %all-gather.11.cloned.1.call-start = ((), (), s32[]{:S(2)}) async-start(), calls=%async_computation.7 | async-start | bytes 2228224 | tf_op jit(solution)/shard_map/all_gather | solution.py:46
  7.9 211.7 %reduce-scatter.2.cloned.1.call-start = ((), (), s32[]{:S(2)}) async-start(), calls=%async_computation.5 | async-start | bytes 4456448 | tf_op jit(solution)/shard_map/reduce_scatter | solution.py:51
  61.3 0.9 copy-start.2
  61.3 9.7 %copy-start.3 = (bf16[1,128,512]{2,1,0:T(8,128)(2,1)S(1)}, bf16[1,128,512]{2,1,0:T(8,128)(2,1)}, u32[]{:S(2)}) copy-start(bf16[1,128,512]{2,1,0:T(8,128)(2,1)} %param.12) | copy-start | bytes 393220
  63.0 128.9 %all-to-all-start.2 = ((bf16[128,16,32]{0,2,1:T(8,128)(2,1)}), bf16[128,16,32]{0,2,1:T(8,128)(2,1)S(1)}, u32[]{:S(2)}, u32[]{:S(2)}) async-start(bf16[128,16,32]{0,2,1:T(8,128)(2,1)} %bitcast.4), calls=%async_computation.2 | async-start | bytes 262144 | tf_op jit(solution)/shard_map/all_to_all | solution.py:62
  180.9 10.0 %copy-start.4 = (bf16[1,128,512]{2,1,0:T(8,128)(2,1)S(1)}, bf16[1,128,512]{2,1,0:T(8,128)(2,1)}, u32[]{:S(2)}) copy-start(bf16[1,128,512]{2,1,0:T(8,128)(2,1)} %param.11) | copy-start | bytes 393220
  191.9 15.9 %all-to-all-start.1 = ((bf16[128,16,32]{0,2,1:T(8,128)(2,1)}), bf16[128,16,32]{0,2,1:T(8,128)(2,1)S(1)}, u32[]{:S(2)}, u32[]{:S(2)}) async-start(bf16[128,16,32]{0,2,1:T(8,128)(2,1)} %bitcast.2), calls=%async_computation.1 | async-start | bytes 262144 | tf_op jit(solution)/shard_map/all_to_all | solution.py:61
  207.8 11.9 %all-to-all-start = ((bf16[128,16,32]{0,2,1:T(8,128)(2,1)}), bf16[128,16,32]{0,2,1:T(8,128)(2,1)S(1)}, u32[]{:S(2)}, u32[]{:S(2)}) async-start(bf16[128,16,32]{0,2,1:T(8,128)(2,1)} %bitcast), calls=%async_computation | async-start | bytes 262144 | tf_op jit(solution)/shard_map/all_to_all | solution.py:60
  211.3 131.9 %all-gather.7.cloned.1.call-start = ((), (), s32[]{:S(2)}) async-start(), calls=%async_computation.4 | async-start | bytes 2228224 | tf_op jit(solution)/shard_map/all_gather | solution.py:97
  221.4 127.9 %all-gather.13.cloned.1.call-start = ((), (), s32[]{:S(2)}) async-start(), calls=%async_computation.8 | async-start | bytes 2228224 | tf_op jit(solution)/shard_map/all_gather | solution.py:47
  222.0 218.7 %all-gather.9.cloned.1.call-start = ((), (), s32[]{:S(2)}) async-start(), calls=%async_computation.6 | async-start | bytes 2228224 | tf_op jit(solution)/shard_map/all_gather | solution.py:98
  343.2 276.3 %all-reduce.6.cloned.1.call-start = ((), (), s32[]{:S(2)}) async-start(), calls=%async_computation.9 | async-start | bytes 4194304 | tf_op jit(solution)/shard_map/psum | solution.py:106
  619.5 2.6 copy-start.1
Sparse Core Ops, SparseCore 0:
  10.1 46.3 all-gather.10
  61.5 105.1 reduce-scatter.1
  221.5 84.2 all-gather.6
  307.8 41.4 all-gather.12
  351.7 88.8 all-gather.8
  445.2 126.5 all-reduce.5
